TPU v7x, 32 devices: a whole 2x2x4 slice. The times are simulated.
32 devices in a mesh: groups: 2 (over y), row: 4 (over x, core), col: 4 (over z).
Axes of the slice: x: 2, y: 2, z: 4, core: 2. Of those that a mesh axis runs over, the one named last changes fastest.
Arguments:
- slope_matrix: bfloat16 [1024, 1024], P(('groups', 'row'), 'col'), parts along dimension 0, may hold values from -0.3125 to 0.3125
- prior_matrix: bfloat16 [1024, 1024], P(('groups', 'row'), 'col'), parts along dimension 0, may hold values from -0.3125 to 0.3125
- slope_blocks: int32 [8, 8], P(('groups', 'row'), 'col'), parts along dimension 0, may hold values from 0 to 23, as said below
- prior_blocks: int32 [8, 8], P(('groups', 'row'), 'col'), parts along dimension 0, may hold values from 0 to 23, as said below
- weight_ids: int32 [512], P(('groups', 'row')), parts along dimension 0, may hold values from 0 to 15
- valid_mask: int32 [512], P(('groups', 'row')), parts along dimension 0, may hold values 0 or 1
- noise_weights: float32 [32], P('groups'), parts along dimension 0, may hold values from 0.25 to 4
- prior_weights: bfloat16 [1024], P(('groups', 'row')), parts along dimension 0, may hold values from 0.19921875 to 2
- frames: float32 [6144, 64], P(('groups', 'row', 'col')), parts along dimension 0, may hold values from -6 to 6
Outputs:
- gram_matrix: float32 [6144, 3072], P(('groups', 'row'), 'col'), parts along dimension 0
- applied: float32 [6144, 64], P(('groups', 'row', 'col')), parts along dimension 0
There are 2 independent parts, one for each index of `groups`. A program takes and returns all parts, laid end to end along the dimension named above; each array names one. Nothing has to cross between parts.
Inputs may be any that keep to these rules, and one draw needn't show every extreme that they name: `slope_blocks`: row i names, for each block-column set c (entries c * 2 to c * 2 + 1), 2 distinct actuator blocks of that set, c * 6 to c * 6 + 5, in the order in which their blocks are stored. `prior_blocks`: row i names, for each block-column set c (entries c * 2 to c * 2 + 1), 2 distinct actuator blocks of that set, c * 6 to c * 6 + 5, in the order in which their blocks are stored.
All inputs are finite; a program needn't handle non-finite values. No bound on the sum of `valid_mask` on one device may be relied on, other than what follows from the above.
Results may differ from a plain program's by a relative error of at most 0.007.
Values may be sent and summed in bfloat16 or wider, within the bound.
No kernel may reach another device: no remote copies, remote signals or barrier semaphores. Data moves between devices by JAX's collectives and lax.ppermute only.
A program may use at most 128 MiB of HBM per device.

v0:
```python
import jax
import jax.numpy as jnp
from jax import lax
from jax.sharding import PartitionSpec as P

BS = 128
AB = 6


def from_root(block, axis, owner):
    block = jnp.where(lax.axis_index(axis) == owner, block, jnp.zeros_like(block))
    return lax.psum(block, axis)


def expand_blocks(values, block_ids, set_index):
    block_count = block_ids.shape[0]
    chosen = block_ids.shape[1]
    targets = set_index * AB + jnp.arange(AB, dtype=jnp.int32)
    onehot = (block_ids[:, :, None] == targets[None, None, :]).astype(jnp.bfloat16)
    shaped = values.reshape(block_count, BS, chosen, BS)
    expanded = jnp.einsum("rskb,rka->rsab", shaped, onehot, preferred_element_type=jnp.float32)
    return expanded.astype(jnp.bfloat16).reshape(block_count * BS, AB * BS)


def shards(
    slope_matrix,
    prior_matrix,
    slope_blocks,
    prior_blocks,
    weight_ids,
    valid_mask,
    noise_weights,
    prior_weights,
    frames,
):
    row_index = lax.axis_index("row")
    col_index = lax.axis_index("col")
    classes = jnp.arange(noise_weights.shape[0], dtype=jnp.int32)
    picked = jnp.sum(
        jnp.where(weight_ids[:, None] == classes[None, :], noise_weights[None, :], 0.0), axis=1
    )
    subap_weight = picked * valid_mask.astype(jnp.float32)
    slope_weight = jnp.repeat(subap_weight, 2).astype(jnp.bfloat16)
    local_rows = jnp.concatenate([slope_matrix, prior_matrix], axis=0)
    local_ids = jnp.concatenate([slope_blocks, prior_blocks], axis=0)
    local_weight = jnp.concatenate([slope_weight, prior_weights], axis=0)
    all_rows, all_ids, all_weight = (
        lax.all_gather(local_rows, "row", axis=0, tiled=True),
        lax.all_gather(local_ids, "row", axis=0, tiled=True),
        lax.all_gather(local_weight, "row", axis=0, tiled=True),
    )
    row_scale = all_weight.astype(jnp.float32)[:, None]
    weighted_rows = (all_rows.astype(jnp.float32) * row_scale).astype(jnp.bfloat16)
    weighted_cols = expand_blocks(weighted_rows, all_ids, col_index)
    sent_rows, sent_ids = (
        from_root(all_rows, "col", row_index),
        from_root(all_ids, "col", row_index),
    )
    row_dense = expand_blocks(sent_rows, sent_ids, row_index)
    gram_tile = lax.dot_general(
        row_dense, weighted_cols, (((0,), (0,)), ((), ())), preferred_element_type=jnp.float32
    )
    frames_rows = lax.all_gather(frames, "col", axis=0, tiled=True)
    frames_cols = from_root(frames_rows, "row", col_index)
    partial_image = jnp.dot(
        gram_tile, frames_cols, precision=lax.Precision.HIGHEST, preferred_element_type=jnp.float32
    )
    applied = lax.psum_scatter(partial_image, "col", scatter_dimension=0, tiled=True)
    return (gram_tile, applied)


def solution(mesh):
    in_specs = (
        P(("groups", "row"), "col"),
        P(("groups", "row"), "col"),
        P(("groups", "row"), "col"),
        P(("groups", "row"), "col"),
        P(("groups", "row")),
        P(("groups", "row")),
        P("groups"),
        P(("groups", "row")),
        P(("groups", "row", "col"), None),
    )
    out_specs = (P(("groups", "row"), "col"), P(("groups", "row", "col"), None))
    return jax.shard_map(shards, mesh=mesh, in_specs=in_specs, out_specs=out_specs, check_vma=False)
```

profile of v0, /device:TPU:0, one launch (start us, length us, event | category | flops | bytes accessed | tf_op | source)
XLA Modules:
  0.0 126.3 jit_solution(12584636910592303553)
XLA Ops:
  7.2 0.0 all-reduce.3.cloned.1.call-start
  7.2 0.9 pad_maximum_fusion
  8.1 8.6 %all_gather.13 = bf16[1024,256]{1,0:T(8,128)(2,1)S(1)} all-gather(bf16[256,256]{1,0:T(8,128)(2,1)S(1)} %pad_maximum_fusion), channel_id=1, replica_groups=mesh['groups'=2,'row'=4,'col'=4] {'row'}, dimensions={0}, use_global_device_ids=true | all-gather | bytes 655360 | tf_op jit(solution)/shard_map/all_gather | solution.py:48
  16.8 0.0 copy-start.8
  16.8 0.9 reshape.31
  17.7 0.0 all-reduce.3.cloned.1.call-update
  17.8 0.0 all-reduce.5.cloned.1.call-start
  17.8 16.0 %all-gather.2 = f32[4,192,64]{1,2,0:T(8,128)S(1)} all-gather(f32[1,192,64]{1,2,0:T(8,128)S(1)} %bitcast.36), channel_id=1, replica_groups=mesh['groups'=2,'row'=4,'col'=4] {'col'}, dimensions={0}, use_global_device_ids=true | all-gather | bytes 245760 | tf_op jit(solution)/shard_map/all_gather | solution.py:63
  33.9 0.2 copy.31
  34.0 0.9 reshape.44
  34.9 0.0 all-reduce.5.cloned.1.call-update
  34.9 0.0 reduce-scatter.4.cloned.1.call-start
  35.0 5.1 %all-gather = s32[4,2,2]{2,1,0:T(2,128)S(1)} all-gather(s32[1,2,2]{2,1,0:T(2,128)S(1)} %add_bitcast_fusion), channel_id=1, replica_groups=mesh['groups'=2,'row'=4,'col'=4] {'row'}, dimensions={0}, use_global_device_ids=true | all-gather | bytes 80 | tf_op jit(solution)/shard_map/all_gather | solution.py:49
  40.1 0.1 copy.34
  40.2 7.8 %psum.21 = s32[8,2]{0,1:T(2,128)S(1)} all-reduce(s32[8,2]{0,1:T(2,128)S(1)} %broadcast_select_fusion.2), channel_id=1, replica_groups=mesh['groups'=2,'row'=4,'col'=4] {'col'}, use_global_device_ids=true, to_apply=%region_0.1 | all-reduce | flops 16 | bytes 128 | tf_op jit(solution)/shard_map/psum | solution.py:12
  47.9 0.1 copy.27
  48.1 0.1 select_reduce_fusion
  48.2 0.1 broadcast_in_dim.32
  48.2 0.2 convert_element_type.38
  48.4 5.1 %all-gather.1 = bf16[4,1,256]{2,1,0:T(2,128)(2,1)S(1)} all-gather(bf16[1,1,256]{2,1,0:T(2,128)(2,1)S(1)} %reshape.37), channel_id=1, replica_groups=mesh['groups'=2,'row'=4,'col'=4] {'row'}, dimensions={0}, use_global_device_ids=true | all-gather | bytes 2560 | tf_op jit(solution)/shard_map/all_gather | solution.py:50
  53.5 0.2 multiply_convert_fusion
  53.7 0.1 reshape.33
  53.8 2.2 %convolution_convert_fusion = bf16[8,6,128,128]{3,1,2,0:T(8,128)(2,1)} fusion(bf16[8,128,2,128]{3,2,1,0:T(2,128)(2,1)S(1)} %reshape.33, s32[6]{0:T(128)S(1)} %iota_add_fusion, s32[8,2]{1,0:T(8,128)S(1)} %bitcast.38), kind=kOutput, calls=%fused_computation | convolution fusion | flops 3932256 | bytes 2097240 | tf_op jit(solution)/shard_map/rskb,rka->rsab/dot_general | solution.py:21
  56.0 3.4 %all-reduce.3.cloned.1.call-done = bf16[8,128,2,128]{3,2,1,0:T(2,128)(2,1)} async-done(((bf16[8,128,2,128]{3,2,1,0:T(2,128)(2,1)}), bf16[8,128,2,128]{3,2,1,0:T(2,128)(2,1)}) %all-reduce.3.cloned.1.call-update) | async-done | bytes 524304 | tf_op jit(solution)/shard_map/psum | solution.py:12
  59.4 2.1 %convolution_convert_fusion.1 = bf16[8,6,128,128]{3,1,2,0:T(8,128)(2,1)S(1)} fusion(bf16[8,128,2,128]{3,2,1,0:T(2,128)(2,1)} %all-reduce.3.cloned.1.call-done, s32[6]{0:T(128)S(1)} %iota_add_fusion.1, s32[8,2]{1,0:T(8,128)S(1)} %copy.27), kind=kOutput, calls=%fused_computation.1 | convolution fusion | flops 3932256 | bytes 2097240 | tf_op jit(solution)/shard_map/rskb,rka->rsab/dot_general | solution.py:21
  61.5 1.5 %fusion = f32[768,768]{1,0:T(8,128)S(1)} fusion(bf16[128,8,6,128]{3,2,1,0:T(8,128)(2,1)S(1)} %bitcast.34, bf16[128,8,6,128]{3,2,1,0:T(8,128)(2,1)S(1)} %bitcast.35), kind=kOutput, calls=%fused_computation.2 | convolution fusion | flops 1207959552 | bytes 5505024 | tf_op jit(solution)/shard_map/dot_general | solution.py:60
  63.0 0.0 copy-start
  63.0 30.5 %all-reduce.5.cloned.1.call-done = f32[768,64]{0,1:T(8,128)} async-done(((f32[768,64]{0,1:T(8,128)}), f32[768,64]{0,1:T(8,128)}) %all-reduce.5.cloned.1.call-update) | async-done | bytes 196624 | tf_op jit(solution)/shard_map/psum | solution.py:12
  93.5 3.7 %fusion.13 = f32[768,64]{1,0:T(8,128)} fusion(f32[768,768]{1,0:T(8,128)S(1)} %fusion, f32[768,64]{0,1:T(8,128)} %all-reduce.5.cloned.1.call-done), kind=kOutput, calls=%fused_computation.27 | convolution fusion | flops 452984832 | bytes 2752512
  97.2 0.0 reduce-scatter.4.cloned.1.call-update
  97.2 21.0 %reduce-scatter.4.cloned.1.call-done = f32[192,64]{1,0:T(8,128)} async-done(((f32[768,64]{1,0:T(8,128)}), f32[192,64]{1,0:T(8,128)}) %reduce-scatter.4.cloned.1.call-update) | async-done | bytes 49168
  118.2 1.6 %copy.38 = f32[192,64]{0,1:T(8,128)} copy(f32[192,64]{1,0:T(8,128)} %reduce-scatter.4.cloned.1.call-done) | data formatting | bytes 98304
  (26 shorter events, 0.1 us)
Async XLA Ops:
  7.2 10.7 %copy-start.2 = (f32[192,64]{0,1:T(8,128)S(1)}, f32[192,64]{0,1:T(8,128)}, u32[]{:S(2)}) copy-start(f32[192,64]{0,1:T(8,128)} %param.17) | copy-start | bytes 147460
  7.2 52.2 %all-reduce.3.cloned.1.call-start = ((), (), s32[]{:S(2)}) async-start(), calls=%async_computation.1 | async-start | bytes 1048576 | tf_op jit(solution)/shard_map/psum | solution.py:12
  16.8 18.2 %copy-start.3 = (s32[1,2]{1,0:T(1,128)S(1)}, s32[1,2]{1,0:T(1,128)}, u32[]{:S(2)}) copy-start(s32[1,2]{1,0:T(1,128)} %param.12) | copy-start | bytes 28
  16.8 18.2 %copy-start.4 = (s32[1,2]{1,0:T(1,128)S(1)}, s32[1,2]{1,0:T(1,128)}, u32[]{:S(2)}) copy-start(s32[1,2]{1,0:T(1,128)} %param.11) | copy-start | bytes 28
  16.8 31.3 %copy-start.5 = (f32[16]{0:T(128)S(1)}, f32[16]{0:T(128)}, u32[]{:S(2)}) copy-start(f32[16]{0:T(128)} %param.15) | copy-start | bytes 196
  16.8 31.3 %copy-start.6 = (s32[64]{0:T(128)S(1)}, s32[64]{0:T(128)}, u32[]{:S(2)}) copy-start(s32[64]{0:T(128)} %param.13) | copy-start | bytes 772
  16.8 31.4 %copy-start.7 = (s32[64]{0:T(128)S(1)}, s32[64]{0:T(128)}, u32[]{:S(2)}) copy-start(s32[64]{0:T(128)} %param.14) | copy-start | bytes 772
  16.8 31.6 %copy-start.8 = (bf16[128]{0:T(256)(128)(2,1)S(1)}, bf16[128]{0:T(256)(128)(2,1)}, u32[]{:S(2)}) copy-start(bf16[128]{0:T(256)(128)(2,1)} %param.16) | copy-start | bytes 772
  17.8 75.8 %all-reduce.5.cloned.1.call-start = ((), (), s32[]{:S(2)}) async-start(), calls=%async_computation.2 | async-start | bytes 393216 | tf_op jit(solution)/shard_map/psum | solution.py:12
  34.9 83.3 %reduce-scatter.4.cloned.1.call-start = ((), (), s32[]{:S(2)}) async-start(), calls=%async_computation.3 | async-start | bytes 491520
  59.4 2.1 %copy-start.1 = (bf16[8,6,128,128]{3,1,2,0:T(8,128)(2,1)S(1)}, bf16[8,6,128,128]{3,1,2,0:T(8,128)(2,1)}, u32[]{:S(2)}) copy-start(bf16[8,6,128,128]{3,1,2,0:T(8,128)(2,1)} %convolution_convert_fusion) | copy-start | bytes 4718596
  63.0 56.8 %copy-start = (f32[768,768]{1,0:T(8,128)}, f32[768,768]{1,0:T(8,128)S(1)}, u32[]{:S(2)}) copy-start(f32[768,768]{1,0:T(8,128)S(1)} %fusion) | copy-start | bytes 7077892
Sparse Core Ops, SparseCore 0:
  17.9 41.4 all-reduce.2
  61.7 31.7 all-reduce.4
  97.3 20.8 reduce-scatter.3
where the time goes:
time: 127 us; the launch traced here: 126 us
  waiting for transfers between devices  54.9 us (43%)
  blocking collectives  42.6 us (34%)
  between operations  13.9 us (11%)
  matrix products  9.43 us (7%)
  local copies, waits for them, and re-layouts  4.09 us (3%)
  other arithmetic  1.28 us (1%)
    psum x2, waiting for transfers between devices, from_root(): return lax.psum(block, axis)  33.9 us
    unnamed x4, waiting for transfers between devices  21 us
    all_gather x1, blocking collectives, shards(): frames_rows = lax.all_gather(frames, 'col', axis=0, tiled=True)  16 us
    all_gather x1, blocking collectives, shards(): lax.all_gather(local_rows, 'row', axis=0, tiled=True)  8.65 us
    psum x1, blocking collectives, from_root(): return lax.psum(block, axis)  7.79 us
    all_gather x1, blocking collectives, shards(): lax.all_gather(local_ids, 'row', axis=0, tiled=True)  5.07 us
    all_gather x1, blocking collectives, shards(): lax.all_gather(local_weight, 'row', axis=0, tiled=True)  5.07 us
    dot_general x2, matrix products, expand_blocks(): jnp.einsum('rskb,rka->rsab', shaped, onehot, preferred_element_type=jnp.f...  4.29 us
  transfers between devices with their start and end apart: 3, of which 3 were waited for; matrix products, arithmetic and copies ran while one was open for 6% of the time, Pallas kernels for 0%

commit v1 on v0

--- a/solution.py
+++ b/solution.py
@@ -5,6 +5,14 @@
 
 BS = 128
 AB = 6
+
+
+def save_types_over_axis(row_data, axis_name):
+    many = jax.lax.axis_size(axis_name)
+    made = [many if p == 0 else 1 for p in range(row_data.ndim)]
+    return jax.lax.all_to_all(
+        jnp.tile(row_data, made), axis_name, split_axis=0, concat_axis=0, tiled=True
+    )
 
 
 def from_root(block, axis, owner):
@@ -45,7 +53,7 @@
     local_ids = jnp.concatenate([slope_blocks, prior_blocks], axis=0)
     local_weight = jnp.concatenate([slope_weight, prior_weights], axis=0)
     all_rows, all_ids, all_weight = (
-        lax.all_gather(local_rows, "row", axis=0, tiled=True),
+        save_types_over_axis(local_rows, "row"),
         lax.all_gather(local_ids, "row", axis=0, tiled=True),
         lax.all_gather(local_weight, "row", axis=0, tiled=True),
     )

time: 127 us -> 132 us (1.039)
  blocking collectives: 42.6 us -> 34.6 us
  waiting for transfers between devices: 54.9 us -> 61.9 us
  starting transfers between devices: 0.12 us -> 4.32 us
    all_to_all x0 -> x1, waiting for transfers between devices: none -> 8.77 us  [save_types_over_axis(): jax.lax.all_to_all(jnp.tile(row_data, made), axis_name, split_axis=0, con...]
    all_gather x1 -> x0, blocking collectives: 8.65 us -> none  [shards(): lax.all_gather(local_rows, 'row', axis=0, tiled=True)]
    all_to_all x0 -> x1, starting transfers between devices: none -> 4.24 us  [save_types_over_axis(): jax.lax.all_to_all(jnp.tile(row_data, made), axis_name, split_axis=0, con...]
    psum x2, waiting for transfers between devices: 33.9 us -> 32.1 us  [from_root(): return lax.psum(block, axis)]
  transfers between devices with their start and end apart: 3 -> 4, of which waited for: 3 -> 4; matrix products, arithmetic and copies ran while one was open for 6% -> 7% of each run, Pallas kernels for 0% -> 0%
where the time goes in v1:
time: 132 us
  waiting for transfers between devices  61.9 us (47%)
  blocking collectives  34.6 us (26%)
  between operations  13.9 us (11%)
  matrix products  10.4 us (8%)
  local copies, waits for them, and re-layouts  5.33 us (4%)
  starting transfers between devices  4.32 us (3%)
    psum x2, waiting for transfers between devices, from_root(): return lax.psum(block, axis)  32.1 us
    unnamed x4, waiting for transfers between devices  21 us
    all_gather x1, blocking collectives, shards(): frames_rows = lax.all_gather(frames, 'col', axis=0, tiled=True)  16.7 us
    all_to_all x1, waiting for transfers between devices, save_types_over_axis(): jax.lax.all_to_all(jnp.tile(row_data, made), axis_name, split_axis=0, con...  8.77 us
    psum x1, blocking collectives, from_root(): return lax.psum(block, axis)  7.76 us
    dot_general x2, matrix products, expand_blocks(): jnp.einsum('rskb,rka->rsab', shaped, onehot, preferred_element_type=jnp.f...  5.32 us
    all_gather x1, blocking collectives, shards(): lax.all_gather(local_ids, 'row', axis=0, tiled=True)  5.07 us
    all_gather x1, blocking collectives, shards(): lax.all_gather(local_weight, 'row', axis=0, tiled=True)  5.07 us
  transfers between devices with their start and end apart: 4, of which 4 were waited for; matrix products, arithmetic and copies ran while one was open for 7% of the time, Pallas kernels for 0%

profile of v1, /device:TPU:0, one launch (start us, length us, event | category | flops | bytes accessed | tf_op | source)
XLA Modules:
  0.0 131.5 jit_solution(13831919034107462326)
XLA Ops:
  7.2 0.9 pad_maximum_fusion
  8.1 0.8 tile.2
  8.9 4.2 %all-to-all-start = ((bf16[4,256,256]{2,1,0:T(8,128)(2,1)}), bf16[4,256,256]{2,1,0:T(8,128)(2,1)S(1)}, u32[]{:S(2)}, u32[]{:S(2)}) async-start(bf16[4,256,256]{2,1,0:T(8,128)(2,1)} %tile.2), calls=%async_computation | async-start | bytes 1048576 | tf_op jit(solution)/shard_map/all_to_all | solution.py:13
  13.2 0.0 copy-start.5
  13.2 0.0 copy-start.6
  13.2 8.8 %all-to-all-done = bf16[4,256,256]{2,1,0:T(8,128)(2,1)S(1)} async-done(((bf16[4,256,256]{2,1,0:T(8,128)(2,1)}), bf16[4,256,256]{2,1,0:T(8,128)(2,1)S(1)}, u32[]{:S(2)}, u32[]{:S(2)}) %all-to-all-start) | async-done | bytes 524320 | tf_op jit(solution)/shard_map/all_to_all | solution.py:13
  22.0 0.9 reshape.48
  22.9 0.0 all-reduce.3.cloned.1.call-update
  22.9 0.0 all-reduce.5.cloned.1.call-start
  23.0 16.7 %all-gather.2 = f32[4,192,64]{1,2,0:T(8,128)S(1)} all-gather(f32[1,192,64]{1,2,0:T(8,128)S(1)} %bitcast.34), channel_id=1, replica_groups=mesh['groups'=2,'row'=4,'col'=4] {'col'}, dimensions={0}, use_global_device_ids=true | all-gather | bytes 245760 | tf_op jit(solution)/shard_map/all_gather | solution.py:71
  39.7 0.2 copy.31
  39.9 0.9 reshape.62
  40.7 0.0 all-reduce.5.cloned.1.call-update
  40.8 0.0 reduce-scatter.4.cloned.1.call-start
  40.8 5.1 %all-gather = s32[4,2,2]{2,1,0:T(2,128)S(1)} all-gather(s32[1,2,2]{2,1,0:T(2,128)S(1)} %add_bitcast_fusion), channel_id=1, replica_groups=mesh['groups'=2,'row'=4,'col'=4] {'row'}, dimensions={0}, use_global_device_ids=true | all-gather | bytes 80 | tf_op jit(solution)/shard_map/all_gather | solution.py:57
  45.9 0.1 copy.34
  46.0 7.8 %psum.21 = s32[8,2]{0,1:T(2,128)S(1)} all-reduce(s32[8,2]{0,1:T(2,128)S(1)} %broadcast_select_fusion.2), channel_id=1, replica_groups=mesh['groups'=2,'row'=4,'col'=4] {'col'}, use_global_device_ids=true, to_apply=%region_0.1 | all-reduce | flops 16 | bytes 128 | tf_op jit(solution)/shard_map/psum | solution.py:20
  53.8 0.1 copy.27
  53.9 0.1 select_reduce_fusion
  54.0 0.1 broadcast_in_dim.32
  54.0 0.2 convert_element_type.42
  54.2 5.1 %all-gather.1 = bf16[4,1,256]{2,1,0:T(2,128)(2,1)S(1)} all-gather(bf16[1,1,256]{2,1,0:T(2,128)(2,1)S(1)} %reshape.56), channel_id=1, replica_groups=mesh['groups'=2,'row'=4,'col'=4] {'row'}, dimensions={0}, use_global_device_ids=true | all-gather | bytes 2560 | tf_op jit(solution)/shard_map/all_gather | solution.py:58
  59.3 0.5 reshape.52
  59.8 3.2 %convolution_convert_fusion = bf16[8,6,128,128]{3,1,2,0:T(8,128)(2,1)} fusion(f32[8,128,2,128]{3,2,1,0:T(2,128)S(1)} %reshape.52, f32[8,128]{1,0:T(8,128)S(1)} %bitcast.37, s32[6]{0:T(128)S(1)} %iota_add_fusion, s32[8,2]{1,0:T(8,128)S(1)} %bitcast.36), kind=kOutput, calls=%fused_computation | convolution fusion | flops 4456544 | bytes 2625624 | tf_op jit(solution)/shard_map/rskb,rka->rsab/dot_general | solution.py:29
  63.0 1.6 %all-reduce.3.cloned.1.call-done = bf16[8,128,2,128]{3,2,1,0:T(2,128)(2,1)} async-done(((bf16[8,128,2,128]{3,2,1,0:T(2,128)(2,1)}), bf16[8,128,2,128]{3,2,1,0:T(2,128)(2,1)}) %all-reduce.3.cloned.1.call-update) | async-done | bytes 524304 | tf_op jit(solution)/shard_map/psum | solution.py:20
  64.6 2.1 %convolution_convert_fusion.1 = bf16[8,6,128,128]{3,1,2,0:T(8,128)(2,1)S(1)} fusion(bf16[8,128,2,128]{3,2,1,0:T(2,128)(2,1)} %all-reduce.3.cloned.1.call-done, s32[6]{0:T(128)S(1)} %iota_add_fusion.1, s32[8,2]{1,0:T(8,128)S(1)} %copy.27), kind=kOutput, calls=%fused_computation.1 | convolution fusion | flops 3932256 | bytes 2097240 | tf_op jit(solution)/shard_map/rskb,rka->rsab/dot_general | solution.py:29
  66.8 1.5 %fusion = f32[768,768]{1,0:T(8,128)S(1)} fusion(bf16[128,8,6,128]{3,2,1,0:T(8,128)(2,1)S(1)} %bitcast.38, bf16[128,8,6,128]{3,2,1,0:T(8,128)(2,1)S(1)} %bitcast.33), kind=kOutput, calls=%fused_computation.2 | convolution fusion | flops 1207959552 | bytes 5505024 | tf_op jit(solution)/shard_map/dot_general | solution.py:68
  68.3 30.5 %all-reduce.5.cloned.1.call-done = f32[768,64]{0,1:T(8,128)} async-done(((f32[768,64]{0,1:T(8,128)}), f32[768,64]{0,1:T(8,128)}) %all-reduce.5.cloned.1.call-update) | async-done | bytes 196624 | tf_op jit(solution)/shard_map/psum | solution.py:20
  98.8 3.6 %fusion.14 = f32[768,64]{1,0:T(8,128)} fusion(f32[768,768]{1,0:T(8,128)S(1)} %fusion, f32[768,64]{0,1:T(8,128)} %all-reduce.5.cloned.1.call-done), kind=kOutput, calls=%fused_computation.28 | convolution fusion | flops 452984832 | bytes 2752512
  102.4 0.0 reduce-scatter.4.cloned.1.call-update
  102.4 20.9 %reduce-scatter.4.cloned.1.call-done = f32[192,64]{1,0:T(8,128)} async-done(((f32[768,64]{1,0:T(8,128)}), f32[192,64]{1,0:T(8,128)}) %reduce-scatter.4.cloned.1.call-update) | async-done | bytes 49168
  123.4 1.6 %copy.38 = f32[192,64]{0,1:T(8,128)} copy(f32[192,64]{1,0:T(8,128)} %reduce-scatter.4.cloned.1.call-done) | data formatting | bytes 98304
  (27 shorter events, 0.1 us)
Async XLA Ops:
  8.0 14.9 %copy-start.1 = (f32[192,64]{0,1:T(8,128)S(1)}, f32[192,64]{0,1:T(8,128)}, u32[]{:S(2)}) copy-start(f32[192,64]{0,1:T(8,128)} %param.17) | copy-start | bytes 147460
  8.9 13.1 %all-to-all-start = ((bf16[4,256,256]{2,1,0:T(8,128)(2,1)}), bf16[4,256,256]{2,1,0:T(8,128)(2,1)S(1)}, u32[]{:S(2)}, u32[]{:S(2)}) async-start(bf16[4,256,256]{2,1,0:T(8,128)(2,1)} %tile.2), calls=%async_computation | async-start | bytes 1048576 | tf_op jit(solution)/shard_map/all_to_all | solution.py:13
  13.1 51.5 %all-reduce.3.cloned.1.call-start = ((), (), s32[]{:S(2)}) async-start(), calls=%async_computation.2 | async-start | bytes 1048576 | tf_op jit(solution)/shard_map/psum | solution.py:20
  13.1 27.7 %copy-start.2 = (s32[1,2]{1,0:T(1,128)S(1)}, s32[1,2]{1,0:T(1,128)}, u32[]{:S(2)}) copy-start(s32[1,2]{1,0:T(1,128)} %param.12) | copy-start | bytes 28
  13.1 27.7 %copy-start.3 = (s32[1,2]{1,0:T(1,128)S(1)}, s32[1,2]{1,0:T(1,128)}, u32[]{:S(2)}) copy-start(s32[1,2]{1,0:T(1,128)} %param.11) | copy-start | bytes 28
  13.1 40.7 %copy-start.4 = (f32[16]{0:T(128)S(1)}, f32[16]{0:T(128)}, u32[]{:S(2)}) copy-start(f32[16]{0:T(128)} %param.15) | copy-start | bytes 196
  13.2 40.7 %copy-start.5 = (s32[64]{0:T(128)S(1)}, s32[64]{0:T(128)}, u32[]{:S(2)}) copy-start(s32[64]{0:T(128)} %param.13) | copy-start | bytes 772
  13.2 40.8 %copy-start.6 = (s32[64]{0:T(128)S(1)}, s32[64]{0:T(128)}, u32[]{:S(2)}) copy-start(s32[64]{0:T(128)} %param.14) | copy-start | bytes 772
  22.0 32.2 %copy-start.7 = (bf16[128]{0:T(256)(128)(2,1)S(1)}, bf16[128]{0:T(256)(128)(2,1)}, u32[]{:S(2)}) copy-start(bf16[128]{0:T(256)(128)(2,1)} %param.16) | copy-start | bytes 772
  22.9 75.8 %all-reduce.5.cloned.1.call-start = ((), (), s32[]{:S(2)}) async-start(), calls=%async_computation.3 | async-start | bytes 393216 | tf_op jit(solution)/shard_map/psum | solution.py:20
  40.8 82.6 %reduce-scatter.4.cloned.1.call-start = ((), (), s32[]{:S(2)}) async-start(), calls=%async_computation.4 | async-start | bytes 491520
  64.6 2.1 %copy-start.8 = (bf16[8,6,128,128]{3,1,2,0:T(8,128)(2,1)S(1)}, bf16[8,6,128,128]{3,1,2,0:T(8,128)(2,1)}, u32[]{:S(2)}) copy-start(bf16[8,6,128,128]{3,1,2,0:T(8,128)(2,1)} %convolution_convert_fusion) | copy-start | bytes 4718596
  68.2 56.7 %copy-start = (f32[768,768]{1,0:T(8,128)}, f32[768,768]{1,0:T(8,128)S(1)}, u32[]{:S(2)}) copy-start(f32[768,768]{1,0:T(8,128)S(1)} %fusion) | copy-start | bytes 7077892
Sparse Core Ops, SparseCore 0:
  23.1 41.5 all-reduce.2
  66.9 31.7 all-reduce.4
  102.6 20.7 reduce-scatter.3
